TPU v7x, 32 devices: a whole 2x2x4 slice. The times are simulated.
32 devices in a mesh: rows: 16 (over z, y, core), cols: 2 (over x).
Axes of the slice: x: 2, y: 2, z: 4, core: 2. Of those that a mesh axis runs over, the one named last changes fastest.
Arguments:
- sketch: bfloat16 [262144, 1024], P('rows', 'cols'), may hold values from -150 to 150
- stiffness: float32 [262144], P('rows'), may hold values from 0.05 to 0.4
- reaction: float32 [262144], P('rows'), may hold values from 0.3 to 3
- panel_order: int32 [8], replicated, may hold values from 0 to 7, each once
Outputs:
- residual: bfloat16 [262144, 1024], P('rows', 'cols')
- basis_rows: bfloat16 [262144, 256], P(('rows', 'cols'))
- factor_cols: float32 [1024, 256], P('cols')
All inputs are finite; a program needn't handle non-finite values.
Results may differ from a plain program's by a relative error of at most 0.0071.
Values may be sent and summed in bfloat16 or wider, within the bound.
No kernel may reach another device: no remote copies, remote signals or barrier semaphores. Data moves between devices by JAX's collectives and lax.ppermute only.
A program may use at most 128 MiB of HBM per device.

v0:
```python
import jax
import jax.numpy as jnp
from jax import lax
from jax.sharding import PartitionSpec as P

PB = 128
NY = 2048


def with_halo(block, sides, width):
    for axis, dim in sides:
        count = lax.axis_size(axis)
        forward = [(i, i + 1) for i in range(count - 1)]
        backward = [(target, source) for source, target in forward]
        low = lax.ppermute(
            lax.slice_in_dim(block, block.shape[dim] - width, None, axis=dim), axis, forward
        )
        high = lax.ppermute(lax.slice_in_dim(block, 0, width, axis=dim), axis, backward)
        block = jnp.concatenate([low, block, high], axis=dim)
    return block


def spread(value, axis, source):
    kept = jnp.where(lax.axis_index(axis) == source, value, 0).astype(value.dtype)
    return lax.psum(kept, axis)


def apply_operator(padded, cell_count, sketch, stiffness, reaction):
    centre = sketch.astype(jnp.float32)
    along_y = jnp.arange(cell_count) % NY
    upward = padded[:cell_count].astype(jnp.float32)
    downward = padded[2 * NY : 2 * NY + cell_count].astype(jnp.float32)
    leftward = jnp.where(
        (along_y == 0)[:, None], 0.0, padded[NY - 1 : NY - 1 + cell_count].astype(jnp.float32)
    )
    rightward = jnp.where(
        (along_y == NY - 1)[:, None], 0.0, padded[NY + 1 : NY + 1 + cell_count].astype(jnp.float32)
    )
    mixing = 4.0 * centre - upward - downward - leftward - rightward
    return (reaction[:, None] * centre + stiffness[:, None] * mixing).astype(jnp.bfloat16)


def factorize(gram_full, first_panel, second_panel, cell_total):
    width_all = gram_full.shape[0]
    positions = jnp.arange(width_all, dtype=jnp.int32)[:, None]
    offsets = jnp.arange(PB, dtype=jnp.int32)[None, :]
    ident_one = (positions == first_panel * PB + offsets).astype(jnp.float32)
    ident_two = (positions == second_panel * PB + offsets).astype(jnp.float32)
    core_block = gram_full / cell_total + jnp.concatenate([ident_one, ident_two], 1)
    diag_one = lax.dynamic_slice_in_dim(core_block[:, :PB], first_panel * PB, PB, 0)
    lower_one = jnp.linalg.cholesky(diag_one)
    identity = jnp.eye(PB, dtype=lower_one.dtype)
    inverse_one = jax.scipy.linalg.solve_triangular(lower_one, identity, lower=True)
    column_one = jnp.dot(core_block[:, :PB], inverse_one.T, precision=lax.Precision.HIGHEST)
    cross_rows = lax.dynamic_slice_in_dim(column_one, second_panel * PB, PB, 0)
    updated = core_block[:, PB:] - jnp.dot(
        column_one, cross_rows.T, precision=lax.Precision.HIGHEST
    )
    diag_two = lax.dynamic_slice_in_dim(updated, second_panel * PB, PB, 0)
    lower_two = jnp.linalg.cholesky(diag_two)
    inverse_two = jax.scipy.linalg.solve_triangular(lower_two, identity, lower=True)
    column_two = jnp.dot(updated, inverse_two.T, precision=lax.Precision.HIGHEST)
    factor = jnp.concatenate([column_one, column_two], 1)
    return (factor, inverse_one, inverse_two, cross_rows)


def solve_basis(panel_one, panel_two, inverse_one, inverse_two, cross_rows):
    basis_one = jnp.dot(
        panel_one, inverse_one.T.astype(jnp.bfloat16), preferred_element_type=jnp.float32
    ).astype(jnp.bfloat16)
    partial_two = (
        panel_two.astype(jnp.float32)
        - jnp.dot(basis_one, cross_rows.T.astype(jnp.bfloat16), preferred_element_type=jnp.float32)
    ).astype(jnp.bfloat16)
    basis_two = jnp.dot(
        partial_two, inverse_two.T.astype(jnp.bfloat16), preferred_element_type=jnp.float32
    ).astype(jnp.bfloat16)
    return jnp.concatenate([basis_one, basis_two], 1)


def per_device(sketch, stiffness, reaction, panel_order):
    cell_count, local_width = sketch.shape
    padded = with_halo(sketch, (("rows", 0),), NY)
    zfield = apply_operator(padded, cell_count, sketch, stiffness, reaction)
    groups = lax.axis_size("cols")
    own_group = lax.axis_index("cols")
    cell_total = cell_count * lax.axis_size("rows")
    first_panel = panel_order[0]
    second_panel = panel_order[1]
    slice_rows = cell_count // groups
    contract_cells = (((0,), (0,)), ((), ()))
    panels_here = local_width // PB

    def own_panel(panel_index):
        return lax.dynamic_slice_in_dim(zfield, panel_index % panels_here * PB, PB, 1)

    panel_one = spread(own_panel(first_panel), "cols", first_panel // panels_here)
    panel_two = spread(own_panel(second_panel), "cols", second_panel // panels_here)
    panels_both = jnp.concatenate([panel_one, panel_two], 1)
    partial_value = lax.dot_general(
        zfield, panels_both, contract_cells, preferred_element_type=jnp.float32
    )
    summed = lax.psum(partial_value, "rows")
    gram_full = lax.all_gather(summed, "cols", axis=0, tiled=True)
    factor, inverse_one, inverse_two, cross_rows = factorize(
        gram_full, first_panel, second_panel, cell_total
    )
    basis_full = solve_basis(panel_one, panel_two, inverse_one, inverse_two, cross_rows)
    own_factor = lax.dynamic_slice_in_dim(factor, own_group * local_width, local_width, 0).astype(
        jnp.bfloat16
    )
    residual = (
        zfield.astype(jnp.float32)
        - jnp.dot(basis_full, own_factor.T, preferred_element_type=jnp.float32)
    ).astype(jnp.bfloat16)
    basis_rows = lax.dynamic_slice_in_dim(basis_full, own_group * slice_rows, slice_rows, 0)
    factor_cols = lax.dynamic_slice_in_dim(factor, own_group * local_width, local_width, 0)
    return (residual, basis_rows, factor_cols)


def solution(mesh):
    return jax.shard_map(
        per_device,
        mesh=mesh,
        in_specs=(P("rows", "cols"), P("rows"), P("rows"), P()),
        out_specs=(P("rows", "cols"), P(("rows", "cols"), None), P("cols", None)),
        check_vma=False,
    )
```

profile of v0, /device:TPU:0, one launch (start us, length us, event | category | flops | bytes accessed | tf_op | source)
XLA Modules:
  0.0 546.9 jit_solution(10395292818311364130)
XLA Ops:
  7.2 0.0 copy-start.3
  7.2 0.0 all-reduce.6.cloned.1.call-start
  7.2 4.5 fusion.40
  11.7 3.7 collective-permute-start
  15.4 1.3 collective-permute-start.1
  16.7 0.0 copy-done.3
  16.7 0.7 fusion.41
  22.4 0.0 collective-permute-done
  22.4 1.7 constant_dynamic-update-slice_fusion.1
  24.1 9.2 %constant_dynamic-update-slice_fusion = (bf16[18432,512]{1,0:T(8,128)(2,1)S(1)}, bf16[18432,512]{1,0:T(8,128)(2,1)S(1)}) fusion(bf16[18432,512]{1,0:T(8,128)(2,1)S(1)} %constant_dynamic-update-slice_fusion.1, bf16[16384,512]{1,0:T(8,128)(2,1)} %param.7), kind=kLoop, calls=%fused_computation.61 | loop fusion | bytes 50331648 | tf_op jit(solution)/shard_map/concatenate | solution.py:19
  33.3 0.0 copy-start
  33.3 0.0 collective-permute-done.1
  33.3 0.1 constant_dynamic-update-slice_fusion.2
  33.5 6.3 %copy-done = bf16[18432,512]{1,0:T(8,128)(2,1)} copy-done((bf16[18432,512]{1,0:T(8,128)(2,1)}, bf16[18432,512]{1,0:T(8,128)(2,1)S(1)}, u32[]{:S(2)}) %copy-start) | copy-done | bytes 18874392
  39.8 36.1 %fusion.1 = bf16[16384,512]{1,0:T(8,128)(2,1)} fusion(bf16[16384,512]{1,0:T(8,128)(2,1)} %param.7, bf16[18432,512]{1,0:T(8,128)(2,1)S(1)} %constant_dynamic-update-slice_fusion.2, bf16[18432,512]{1,0:T(8,128)(2,1)} %copy-done, f32[16384]{0:T(1024)} %param.8, f32[16384]{0:T(1024)} %param.9, pred[16384]{0:T(1024)(128)(4,1)S(1)} %get-tuple-element.18, ...), kind=kLoop, calls=%fused_computation.3 | loop fusion | flops 134217728 | bytes 100827136 | tf_op jit(solution)/shard_map/convert_element_type | solution.py:40
  75.8 6.4 %dynamic-slice_select_fusion = (bf16[16384,128]{1,0:T(8,128)(2,1)}, bf16[16384,128]{1,0:T(8,128)(2,1)}) fusion(bf16[16384,512]{1,0:T(8,128)(2,1)} %fusion.1, s32[]{:T(128)S(6)} %select_n.88, pred[]{:T(512)S(6)} %eq.61, s32[]{:T(128)S(6)} %select_n.83, pred[]{:T(512)S(6)} %eq.60), kind=kLoop, calls=%fused_computation.22 | loop fusion | flops 4194304 | bytes 16777226 | tf_op jit(solution)/shard_map/jit(_where)/select_n | solution.py:24
  82.2 0.0 all-reduce.6.cloned.1.call-update
  82.3 0.0 all-reduce.4.cloned.1.call-start
  82.3 239.8 %all-reduce.6.cloned.1.call-done = (bf16[16384,128]{1,0:T(8,128)(2,1)}, bf16[16384,128]{1,0:T(8,128)(2,1)}) async-done(((bf16[16384,128]{1,0:T(8,128)(2,1)}, bf16[16384,128]{1,0:T(8,128)(2,1)}), (bf16[16384,128]{1,0:T(8,128)(2,1)}, bf16[16384,128]{1,0:T(8,128)(2,1)})) %all-reduce.6.cloned.1.call-update) | async-done | bytes 8388624 | tf_op jit(solution)/shard_map/psum | solution.py:25
  322.1 13.6 %fusion.8 = f32[512,256]{0,1:T(8,128)} fusion(bf16[16384,512]{1,0:T(8,128)(2,1)} %fusion.1, bf16[16384,128]{1,0:T(8,128)(2,1)} %get-tuple-element.9, bf16[16384,128]{1,0:T(8,128)(2,1)} %get-tuple-element.8), kind=kOutput, calls=%fused_computation.17 | convolution fusion | flops 4311744512 | bytes 25690112 | tf_op jit(solution)/shard_map/dot_general | solution.py:100
  335.6 0.0 all-reduce.4.cloned.1.call-update
  335.6 0.2 all-gather.2.cloned.1.call-start
  335.9 90.3 %all-reduce.4.cloned.1.call-done = f32[512,256]{0,1:T(8,128)} async-done(((f32[512,256]{0,1:T(8,128)}), f32[512,256]{0,1:T(8,128)}) %all-reduce.4.cloned.1.call-update) | async-done | bytes 524304 | tf_op jit(solution)/shard_map/psum | solution.py:103
  426.2 0.0 all-gather.2.cloned.1.call-update
  427.5 0.2 iota_compare_fusion
  427.7 21.9 %all-gather.2.cloned.1.call-done = f32[1024,256]{0,1:T(8,128)} async-done(((f32[512,256]{0,1:T(8,128)}), f32[1024,256]{0,1:T(8,128)}) %all-gather.2.cloned.1.call-update) | async-done | bytes 1048592 | tf_op jit(solution)/shard_map/all_gather | solution.py:104
  449.6 1.4 convert_add_fusion
  451.0 0.1 copy.8
  451.2 11.7 %cholesky.44 = f32[128,128]{1,0:T(8,128)S(1)} custom-call(f32[128,128]{1,0:T(8,128)S(1)} %fusion.24), custom_call_target="Cholesky" | custom-call | tf_op jit(solution)/shard_map/jit(cholesky)/cholesky | solution.py:51
  462.9 0.6 compare_reduce_fusion.1
  463.5 0.7 fusion.19
  464.2 9.8 %custom-call.6 = f32[1,128,128]{1,2,0:T(8,128)S(1)} custom-call(f32[1,128,128]{2,1,0:T(8,128)S(1)} %fusion.19), custom_call_target="InvertDiagBlocksLowerTriangular" | custom-call | tf_op jit(solution)/shard_map/jit(_solve_triangular)/triangular_solve | solution.py:53
  474.0 0.3 fusion.17
  474.3 5.5 convolution_convert_fusion.1
  479.8 0.6 fusion.38
  480.4 0.6 convolution_subtract_fusion.1
  481.1 0.1 copy.10
  481.2 11.9 %cholesky.55 = f32[128,128]{1,0:T(8,128)S(1)} custom-call(f32[128,128]{1,0:T(8,128)S(1)} %fusion.22), custom_call_target="Cholesky" | custom-call | tf_op jit(solution)/shard_map/jit(cholesky)/cholesky | solution.py:60
  493.1 0.6 compare_reduce_fusion
  493.7 0.7 fusion.20
  494.4 9.8 %custom-call.7 = f32[1,128,128]{1,2,0:T(8,128)S(1)} custom-call(f32[1,128,128]{2,1,0:T(8,128)S(1)} %fusion.20), custom_call_target="InvertDiagBlocksLowerTriangular" | custom-call | tf_op jit(solution)/shard_map/jit(_solve_triangular)/triangular_solve | solution.py:61
  504.2 0.3 fusion.15
  504.5 0.6 fusion.42
  505.1 8.0 %convolution_convert_fusion = bf16[16384,128]{0,1:T(8,128)(2,1)} fusion(bf16[16384,128]{0,1:T(8,128)(2,1)} %convolution_convert_fusion.1, bf16[16384,128]{1,0:T(8,128)(2,1)} %get-tuple-element.9, f32[1024,128]{0,1:T(8,128)S(1)} %fusion.38, s32[]{:T(128)S(6)} %select_n.91, f32[128,128]{1,0:T(8,128)S(1)} %fusion.15), kind=kOutput, calls=%fused_computation.12 | convolution fusion | flops 1082146816 | bytes 12681220 | tf_op jit(solution)/shard_map/dot_general | solution.py:75
  513.1 1.0 copy.12
  514.1 0.0 copy-start.1
  514.1 0.0 copy-start.2
  514.1 17.7 %subtract_convert_fusion = bf16[16384,512]{1,0:T(8,128)(2,1)} fusion(bf16[16384,512]{1,0:T(8,128)(2,1)} %fusion.1, bf16[16384,128]{0,1:T(8,128)(2,1)} %convolution_convert_fusion, bf16[16384,128]{0,1:T(8,128)(2,1)} %convolution_convert_fusion.1, f32[512,256]{0,1:T(8,128)S(1)} %fusion.13), kind=kOutput, calls=%fused_computation.9 | convolution fusion | flops 4337041408 | bytes 42467328 | tf_op jit(solution)/shard_map/dot_general | solution.py:114
  531.8 0.0 copy-done.1
  531.8 0.0 copy-done.2
  531.8 2.2 fusion.12
  534.0 6.4 %copy.11 = bf16[8192,256]{1,0:T(8,128)(2,1)} copy(bf16[8192,256]{0,1:T(8,128)(2,1)} %fusion.12) | data formatting | bytes 8388608
  (11 shorter events, 0.3 us)
Async XLA Ops:
  7.2 9.5 %copy-start.3 = (s32[8]{0:T(128)S(1)}, s32[8]{0:T(128)}, u32[]{:S(2)}) copy-start(s32[8]{0:T(128)} %param.10) | copy-start | bytes 100
  7.2 314.9 %all-reduce.6.cloned.1.call-start = ((), (), s32[]{:S(2)}) async-start(), calls=%async_computation.2 | async-start | bytes 16777216 | tf_op jit(solution)/shard_map/psum | solution.py:25
  11.7 10.7 %collective-permute-start = (bf16[2048,512]{1,0:T(8,128)(2,1)}, bf16[2048,512]{1,0:T(8,128)(2,1)}, u32[]{:S(2)}, u32[]{:S(2)}) collective-permute-start(bf16[2048,512]{1,0:T(8,128)(2,1)} %get-tuple-element.14), channel_id=1, source_target_pairs={{0,2},{2,4},{4,6},{6,8},{8,10},{10,12},{12,14},{14,16},{16,18},{18... | collective-permute-start | bytes 6291464 | tf_op jit(solution)/shard_map/ppermute | solution.py:15
  15.4 17.9 %collective-permute-start.1 = (bf16[2048,512]{1,0:T(8,128)(2,1)}, bf16[2048,512]{1,0:T(8,128)(2,1)S(1)}, u32[]{:S(2)}, u32[]{:S(2)}) collective-permute-start(bf16[2048,512]{1,0:T(8,128)(2,1)} %get-tuple-element.15), channel_id=1, source_target_pairs={{2,0},{4,2},{6,4},{8,6},{10,8},{12,10},{14,12},{16,14},{18,16},{20... | collective-permute-start | bytes 6291464 | tf_op jit(solution)/shard_map/ppermute | solution.py:18
  33.3 6.5 %copy-start = (bf16[18432,512]{1,0:T(8,128)(2,1)}, bf16[18432,512]{1,0:T(8,128)(2,1)S(1)}, u32[]{:S(2)}) copy-start(bf16[18432,512]{1,0:T(8,128)(2,1)S(1)} %get-tuple-element.12) | copy-start | bytes 56623108
  82.3 343.9 %all-reduce.4.cloned.1.call-start = ((), (), s32[]{:S(2)}) async-start(), calls=%async_computation | async-start | bytes 1048576 | tf_op jit(solution)/shard_map/psum | solution.py:103
  335.6 113.9 %all-gather.2.cloned.1.call-start = ((), (), s32[]{:S(2)}) async-start(), calls=%async_computation.1 | async-start | bytes 1572864 | tf_op jit(solution)/shard_map/all_gather | solution.py:104
  514.1 17.7 %copy-start.1 = (bf16[16384,128]{0,1:T(8,128)(2,1)S(1)}, bf16[16384,128]{0,1:T(8,128)(2,1)}, u32[]{:S(2)}) copy-start(bf16[16384,128]{0,1:T(8,128)(2,1)} %convolution_convert_fusion.1) | copy-start | bytes 12582916
  514.1 17.7 %copy-start.2 = (bf16[16384,128]{0,1:T(8,128)(2,1)S(1)}, bf16[16384,128]{0,1:T(8,128)(2,1)}, u32[]{:S(2)}) copy-start(bf16[16384,128]{0,1:T(8,128)(2,1)} %convolution_convert_fusion) | copy-start | bytes 12582916
Sparse Core Ops, SparseCore 0:
  82.4 239.6 all-reduce.5
  335.8 90.3 all-reduce.3
  427.7 21.7 all-gather.1
where the time goes:
time: 547 us
  waiting for transfers between devices  352 us (64%)
  other arithmetic  92.2 us (17%)
  matrix products  47.1 us (9%)
  local copies, waits for them, and re-layouts  30.1 us (6%)
  between operations  20.2 us (4%)
    psum x1, waiting for transfers between devices, spread(): return lax.psum(kept, axis)  240 us
    psum x1, waiting for transfers between devices, per_device(): summed = lax.psum(partial_value, 'rows')  90.3 us
    convert_element_type x1, other arithmetic, apply_operator(): (reaction[:, None] * centre + stiffness[:, None] * mixing).astype(jnp.bfl...  36.1 us
    all_gather x1, waiting for transfers between devices, per_device(): gram_full = lax.all_gather(summed, 'cols', axis=0, tiled=True)  21.9 us
    dot_general x1, matrix products, per_device(): jnp.dot(basis_full, own_factor.T, preferred_element_type=jnp.float32)  17.7 us
    unnamed x11, local copies, waits for them, and re-layouts  15.4 us
    dot_general x1, matrix products, per_device(): lax.dot_general(zfield, panels_both, contract_cells, preferred_element_ty...  13.6 us
    another operation x3, other arithmetic, factorize(): lower_two = jnp.linalg.cholesky(diag_two)  12.6 us
  transfers between devices with their start and end apart: 5, of which 3 were waited for; matrix products, arithmetic and copies ran while one was open for 2% of the time, Pallas kernels for 0%

commit v1 on v0

--- a/solution.py
+++ b/solution.py
@@ -1,10 +1,21 @@
 import jax
 import jax.numpy as jnp
 from jax import lax
+from jax.experimental import pallas as pl
+from jax.experimental.pallas import tpu as pltpu
 from jax.sharding import PartitionSpec as P
 
 PB = 128
 NY = 2048
+LANES = 128
+BF16 = jnp.bfloat16
+F32 = jnp.float32
+HIGHEST = lax.Precision.HIGHEST
+SWAP = [(0, 1), (1, 0)]
+VMEM_BYTES = 56 << 20
+LITTLE = pl.CostEstimate(flops=1 << 20, bytes_accessed=1 << 14, transcendentals=0)
+CELLS_FIRST = (((0,), (0,)), ((), ()))
+LAST_LAST = (((1,), (1,)), ((), ()))
 
 
 def with_halo(block, sides, width):
@@ -51,34 +62,32 @@
     lower_one = jnp.linalg.cholesky(diag_one)
     identity = jnp.eye(PB, dtype=lower_one.dtype)
     inverse_one = jax.scipy.linalg.solve_triangular(lower_one, identity, lower=True)
-    column_one = jnp.dot(core_block[:, :PB], inverse_one.T, precision=lax.Precision.HIGHEST)
+    column_one = jnp.dot(core_block[:, :PB], inverse_one.T, precision=HIGHEST)
     cross_rows = lax.dynamic_slice_in_dim(column_one, second_panel * PB, PB, 0)
-    updated = core_block[:, PB:] - jnp.dot(
-        column_one, cross_rows.T, precision=lax.Precision.HIGHEST
-    )
+    updated = core_block[:, PB:] - jnp.dot(column_one, cross_rows.T, precision=HIGHEST)
     diag_two = lax.dynamic_slice_in_dim(updated, second_panel * PB, PB, 0)
     lower_two = jnp.linalg.cholesky(diag_two)
     inverse_two = jax.scipy.linalg.solve_triangular(lower_two, identity, lower=True)
-    column_two = jnp.dot(updated, inverse_two.T, precision=lax.Precision.HIGHEST)
+    column_two = jnp.dot(updated, inverse_two.T, precision=HIGHEST)
     factor = jnp.concatenate([column_one, column_two], 1)
     return (factor, inverse_one, inverse_two, cross_rows)
 
 
 def solve_basis(panel_one, panel_two, inverse_one, inverse_two, cross_rows):
     basis_one = jnp.dot(
-        panel_one, inverse_one.T.astype(jnp.bfloat16), preferred_element_type=jnp.float32
-    ).astype(jnp.bfloat16)
+        panel_one, inverse_one.T.astype(BF16), preferred_element_type=F32
+    ).astype(BF16)
     partial_two = (
-        panel_two.astype(jnp.float32)
-        - jnp.dot(basis_one, cross_rows.T.astype(jnp.bfloat16), preferred_element_type=jnp.float32)
-    ).astype(jnp.bfloat16)
+        panel_two.astype(F32)
+        - jnp.dot(basis_one, cross_rows.T.astype(BF16), preferred_element_type=F32)
+    ).astype(BF16)
     basis_two = jnp.dot(
-        partial_two, inverse_two.T.astype(jnp.bfloat16), preferred_element_type=jnp.float32
-    ).astype(jnp.bfloat16)
+        partial_two, inverse_two.T.astype(BF16), preferred_element_type=F32
+    ).astype(BF16)
     return jnp.concatenate([basis_one, basis_two], 1)
 
 
-def per_device(sketch, stiffness, reaction, panel_order):
+def any_groups(sketch, stiffness, reaction, panel_order):
     cell_count, local_width = sketch.shape
     padded = with_halo(sketch, (("rows", 0),), NY)
     zfield = apply_operator(padded, cell_count, sketch, stiffness, reaction)
@@ -88,7 +97,6 @@
     first_panel = panel_order[0]
     second_panel = panel_order[1]
     slice_rows = cell_count // groups
-    contract_cells = (((0,), (0,)), ((), ()))
     panels_here = local_width // PB
 
     def own_panel(panel_index):
@@ -97,9 +105,7 @@
     panel_one = spread(own_panel(first_panel), "cols", first_panel // panels_here)
     panel_two = spread(own_panel(second_panel), "cols", second_panel // panels_here)
     panels_both = jnp.concatenate([panel_one, panel_two], 1)
-    partial_value = lax.dot_general(
-        zfield, panels_both, contract_cells, preferred_element_type=jnp.float32
-    )
+    partial_value = lax.dot_general(zfield, panels_both, CELLS_FIRST, preferred_element_type=F32)
     summed = lax.psum(partial_value, "rows")
     gram_full = lax.all_gather(summed, "cols", axis=0, tiled=True)
     factor, inverse_one, inverse_two, cross_rows = factorize(
@@ -107,15 +113,809 @@
     )
     basis_full = solve_basis(panel_one, panel_two, inverse_one, inverse_two, cross_rows)
     own_factor = lax.dynamic_slice_in_dim(factor, own_group * local_width, local_width, 0).astype(
-        jnp.bfloat16
+        BF16
     )
     residual = (
-        zfield.astype(jnp.float32)
-        - jnp.dot(basis_full, own_factor.T, preferred_element_type=jnp.float32)
-    ).astype(jnp.bfloat16)
+        zfield.astype(F32) - jnp.dot(basis_full, own_factor.T, preferred_element_type=F32)
+    ).astype(BF16)
     basis_rows = lax.dynamic_slice_in_dim(basis_full, own_group * slice_rows, slice_rows, 0)
     factor_cols = lax.dynamic_slice_in_dim(factor, own_group * local_width, local_width, 0)
     return (residual, basis_rows, factor_cols)
+
+
+def column_of(row):
+    return jnp.transpose(jnp.broadcast_to(row, (LANES, LANES)))
+
+
+WIDE = LANES + 32
+PIECES = NY // LANES
+
+
+def beside(lead):
+    row = lax.broadcasted_iota(jnp.int32, (LANES, WIDE), 0) + lead
+    col = lax.broadcasted_iota(jnp.int32, (LANES, WIDE), 1)
+    return jnp.where((col == row - 1) | (col == row + 1), 1.0, 0.0).astype(BF16)
+
+
+def stencil_piece(number, load, above, below, mix_col, stiff_col):
+    lead = 0 if number == 0 else 32 if number == PIECES - 1 else 16
+    wide = load(number * LANES - lead, WIDE)
+    sides = jnp.dot(beside(lead), wide, preferred_element_type=F32)
+    around = (above.astype(F32) + below.astype(F32)) + sides
+    centre = load(number * LANES, LANES).astype(F32)
+    return (mix_col * centre - stiff_col * around).astype(BF16)
+
+
+def panel_lines(sketch, mix, stiff, info, jobs, line_of, tile_of, low=None, high=None):
+    last_line = sketch.shape[0] // NY - 1
+
+    def body(info_ref, up_ref, mid_ref, down_ref, mix_ref, stiff_ref, *rest):
+        out_ref = rest[-1]
+
+        def run(above, below):
+            for number in range(PIECES):
+                at = slice(number * LANES, (number + 1) * LANES)
+                out_ref[at, :] = stencil_piece(
+                    number,
+                    lambda start, size: mid_ref[start : start + size, :],
+                    above[at, :],
+                    below[at, :],
+                    column_of(mix_ref[number : number + 1, :]),
+                    column_of(stiff_ref[number : number + 1, :]),
+                )
+
+        if low is None:
+            run(up_ref, down_ref)
+        else:
+            line = line_of(pl.program_id(0), info_ref)
+
+            @pl.when(line == 0)
+            def _():
+                run(rest[0], down_ref)
+
+            @pl.when(line == last_line)
+            def _():
+                run(up_ref, rest[1])
+
+    def block(shift):
+        return pl.BlockSpec(
+            (NY, LANES),
+            lambda j, t: (jnp.clip(line_of(j, t) + shift, 0, last_line), tile_of(j, t)),
+        )
+
+    coef = pl.BlockSpec((PIECES, LANES), lambda j, t: (line_of(j, t), 0))
+    halo = pl.BlockSpec((NY, LANES), lambda j, t: (0, 0))
+    extra = [] if low is None else [low, high]
+    return pl.pallas_call(
+        body,
+        grid_spec=pltpu.PrefetchScalarGridSpec(
+            num_scalar_prefetch=1,
+            grid=(jobs,),
+            in_specs=[block(-1), block(0), block(1), coef, coef] + [halo] * len(extra),
+            out_specs=pl.BlockSpec((NY, LANES), lambda j, t: (0, j)),
+        ),
+        out_shape=jax.ShapeDtypeStruct((NY, jobs * LANES), BF16),
+        compiler_params=pltpu.CompilerParams(vmem_limit_bytes=VMEM_BYTES),
+        cost_estimate=LITTLE,
+        name="panel_lines",
+    )(info, sketch, sketch, sketch, mix, stiff, *extra)
+
+
+def field_part(sketch, mix, stiff, info, panels, jobs, stride, line_of, sources, base=None):
+    cells, width = sketch.shape
+    arrays = []
+    for copies in sources:
+        for array, *_ in copies:
+            if not any(array is known for known in arrays):
+                arrays.append(array)
+    index = lambda array: [array is known for known in arrays].index(True)
+    plan = [
+        (slot, index(array), row, column, size, place)
+        for slot, copies in enumerate(sources)
+        for array, row, column, size, place in copies
+    ]
+
+    def body(info_ref, *refs):
+        hbm, rest = refs[: len(arrays)], refs[len(arrays) :]
+        mix_ref, stiff_ref = rest[:2]
+        z_ref, gram_ref, lines_ref, acc_ref, sems = rest[-5:]
+        step = pl.program_id(0)
+
+        def copy_of(number):
+            slot, which, row, column, size, place = plan[number]
+            at = place(info_ref)
+            at = at if isinstance(at, int) else pl.multiple_of(at, LANES)
+            return pltpu.make_async_copy(
+                hbm[which].at[row : row + NY, column : column + size],
+                lines_ref.at[slot, :, pl.ds(at, size)],
+                sems.at[number],
+            )
+
+        def wait_for(slots):
+            for number, entry in enumerate(plan):
+                if entry[0] in slots:
+                    copy_of(number).wait()
+
+        @pl.when(step == 0)
+        def _():
+            for number in range(len(plan)):
+                copy_of(number).start()
+            wait_for((0, 1, 2))
+
+        for job in range(1, jobs):
+
+            @pl.when(step == job)
+            def _():
+                wait_for([stride * job + k for k in range(3) if k >= 3 - stride])
+
+        first = step * stride
+        for number in range(PIECES):
+            at = slice(number * LANES, (number + 1) * LANES)
+            mix_col = column_of(mix_ref[number : number + 1, :])
+            stiff_col = column_of(stiff_ref[number : number + 1, :])
+            for tile in range(width // LANES):
+                cols = slice(tile * LANES, (tile + 1) * LANES)
+                z_ref[at, cols] = stencil_piece(
+                    number,
+                    lambda start, size: lines_ref[first + 1, start : start + size, cols],
+                    lines_ref[first, at, cols],
+                    lines_ref[first + 2, at, cols],
+                    mix_col,
+                    stiff_col,
+                )
+
+        own = [
+            z_ref[:, pl.ds(pl.multiple_of(info_ref[1 + k] * PB, PB), PB)] for k in range(panels)
+        ]
+        own = own[0] if panels == 1 else jnp.concatenate(own, 1)
+        product = lax.dot_general(own, z_ref[...], CELLS_FIRST, preferred_element_type=F32)
+
+        @pl.when(step == 0)
+        def _():
+            acc_ref[...] = product
+
+        @pl.when(step > 0)
+        def _():
+            acc_ref[...] += product
+
+        @pl.when(step == jobs - 1)
+        def _():
+            gram_ref[...] = jnp.transpose(acc_ref[...])
+
+    coef = pl.BlockSpec((PIECES, LANES), lambda j, t: (line_of(j, t), 0))
+    ANY = pl.BlockSpec(memory_space=pl.ANY)
+    extra = [] if base is None else [base]
+    return pl.pallas_call(
+        body,
+        grid_spec=pltpu.PrefetchScalarGridSpec(
+            num_scalar_prefetch=1,
+            grid=(jobs,),
+            in_specs=[ANY] * len(arrays) + [coef, coef] + [ANY] * len(extra),
+            out_specs=[
+                pl.BlockSpec((NY, width), lambda j, t: (line_of(j, t), 0)),
+                pl.BlockSpec((width, panels * PB), lambda j, t: (0, 0)),
+            ],
+            scratch_shapes=[
+                pltpu.VMEM((len(sources), NY, width), BF16),
+                pltpu.VMEM((panels * PB, width), F32),
+                pltpu.SemaphoreType.DMA((len(plan),)),
+            ],
+        ),
+        out_shape=[
+            jax.ShapeDtypeStruct((cells, width), BF16),
+            jax.ShapeDtypeStruct((width, panels * PB), F32),
+        ],
+        input_output_aliases={} if base is None else {3 + len(arrays): 0},
+        compiler_params=pltpu.CompilerParams(vmem_limit_bytes=VMEM_BYTES),
+        cost_estimate=LITTLE,
+        name="field_part",
+    )(info, *arrays, mix, stiff, *extra)
+
+
+def whole_field(sketch, mix, stiff, info, panels, low, high):
+    width = sketch.shape[1]
+    lines = sketch.shape[0] // NY
+
+    def line(number):
+        return [(sketch, number * NY, 0, width, lambda t: 0)]
+
+    field, gram = field_part(
+        sketch,
+        mix,
+        stiff,
+        info,
+        panels,
+        lines - 2,
+        1,
+        lambda j, t: j + 1,
+        [line(k) for k in range(lines)],
+    )
+    field, more = field_part(
+        sketch,
+        mix,
+        stiff,
+        info,
+        panels,
+        2,
+        3,
+        lambda j, t: j * (lines - 1),
+        [low, line(0), line(1), line(lines - 2), line(lines - 1), high],
+        field,
+    )
+    return field, gram + more
+
+
+def copy_lines(source, info, jobs, line_of, tile_of, width=LANES):
+    def body(info_ref, z_ref, out_ref):
+        out_ref[...] = z_ref[...]
+
+    return pl.pallas_call(
+        body,
+        grid_spec=pltpu.PrefetchScalarGridSpec(
+            num_scalar_prefetch=1,
+            grid=(jobs,),
+            in_specs=[pl.BlockSpec((NY, width), lambda j, t: (line_of(j, t), tile_of(j, t)))],
+            out_specs=pl.BlockSpec((NY, width), lambda j, t: (0, j)),
+        ),
+        out_shape=jax.ShapeDtypeStruct((NY, jobs * width), BF16),
+        compiler_params=pltpu.CompilerParams(vmem_limit_bytes=VMEM_BYTES),
+        cost_estimate=LITTLE,
+        name="copy_lines",
+    )(info, source)
+
+
+def gram_lines(zfield, others, info, jobs, line_of):
+    width = zfield.shape[1]
+    total = sum(columns for _, columns, _ in others)
+
+    def body(info_ref, z_ref, *rest):
+        out_ref, acc_ref = rest[-2:]
+        step = pl.program_id(0)
+        parts = [ref[...] for ref in rest[:-2]]
+        right = parts[0] if len(parts) == 1 else jnp.concatenate(parts, 1)
+        product = lax.dot_general(right, z_ref[...], CELLS_FIRST, preferred_element_type=F32)
+
+        @pl.when(step == 0)
+        def _():
+            acc_ref[...] = product
+
+        @pl.when(step > 0)
+        def _():
+            acc_ref[...] += product
+
+        @pl.when(step == jobs - 1)
+        def _():
+            out_ref[...] = jnp.transpose(acc_ref[...])
+
+    return pl.pallas_call(
+        body,
+        grid_spec=pltpu.PrefetchScalarGridSpec(
+            num_scalar_prefetch=1,
+            grid=(jobs,),
+            in_specs=[pl.BlockSpec((NY, width), lambda j, t: (line_of(j, t), 0))]
+            + [pl.BlockSpec((NY, columns), block) for _, columns, block in others],
+            out_specs=pl.BlockSpec((width, total), lambda j, t: (0, 0)),
+            scratch_shapes=[pltpu.VMEM((total, width), F32)],
+        ),
+        out_shape=jax.ShapeDtypeStruct((width, total), F32),
+        compiler_params=pltpu.CompilerParams(vmem_limit_bytes=VMEM_BYTES),
+        cost_estimate=LITTLE,
+        name="gram_lines",
+    )(info, zfield, *[array for array, _, _ in others])
+
+
+def inverse_factor(block):
+    def body(a_ref, o_ref, work):
+        sub = lax.broadcasted_iota(jnp.int32, (8, PB), 0)
+        row = lax.broadcasted_iota(jnp.int32, (PB, PB), 0)
+        lane = lax.broadcasted_iota(jnp.int32, (PB, PB), 1)
+        work[:, :PB] = a_ref[...]
+        work[:, PB:] = (row == lane).astype(F32)
+
+        def spread_row(value, s):
+            return jnp.broadcast_to(value[s : s + 1, :], (8, PB))
+
+        @pl.loop(0, PB // 8)
+        def _(step):
+            at = pl.ds(pl.multiple_of(step * 8, 8), 8)
+            left, right = work[at, :PB], work[at, PB:]
+            near = pltpu.roll(left, (PB - step * 8) % PB, 1)
+            columns = [jnp.broadcast_to(near[:, c : c + 1], (8, PB)) for c in range(8)]
+            for s in range(8):
+                scale = lax.rsqrt(spread_row(columns[s], s))
+                row_left = spread_row(left, s) * scale
+                row_right = spread_row(right, s) * scale
+                weight = jnp.where(sub > s, columns[s] * scale, 0.0)
+                left = jnp.where(sub == s, row_left, left - weight * row_left)
+                right = jnp.where(sub == s, row_right, right - weight * row_right)
+                for c in range(s + 1, 8):
+                    columns[c] = columns[c] - weight * (spread_row(columns[s], c) * scale)
+            o_ref[at, :] = right
+            both = jnp.concatenate([left, right], 1)
+            work[...] -= lax.dot_general(
+                left, both, CELLS_FIRST, precision=HIGHEST, preferred_element_type=F32
+            )
+
+    return pl.pallas_call(
+        body,
+        out_shape=jax.ShapeDtypeStruct((PB, PB), F32),
+        scratch_shapes=[pltpu.VMEM((PB, 2 * PB), F32)],
+        cost_estimate=LITTLE,
+        name="inverse_factor",
+    )(block)
+
+
+def finish(zfield, chunks, solves, factor, info, pair, slot_of):
+    cells, width = zfield.shape
+    lines = cells // NY
+    block = 2 * PB if pair else PB
+    arrays = []
+    for array, _ in chunks:
+        if not any(array is known for known in arrays):
+            arrays.append(array)
+    index = lambda array: [array is known for known in arrays].index(True)
+
+    def body(t, *refs):
+        hbm, rest = refs[: len(arrays)], refs[len(arrays) :]
+        z_ref, one_ref, cross_ref, two_ref, f_ref, out_ref, half_ref = rest[:7]
+        got_ref, pan_ref, bas_ref, sems = rest[7:]
+        step = pl.program_id(0)
+        role = t[0]
+
+        def copy_of(slot):
+            array, column = chunks[slot]
+            return pltpu.make_async_copy(
+                hbm[index(array)].at[:, column : column + block], got_ref.at[slot], sems.at[slot]
+            )
+
+        @pl.when(step == 0)
+        def _():
+            for slot in range(lines):
+                copy_of(slot).start()
+
+        mine = slot_of(step, t)
+        for slot in range(lines):
+
+            @pl.when(mine == slot)
+            def _():
+                copy_of(slot).wait()
+
+        def tile(which):
+            return z_ref[:, pl.ds(pl.multiple_of(t[which] * PB, PB), PB)]
+
+        @pl.when(role == 0)
+        def _():
+            pan_ref[:, :PB] = tile(1)
+            pan_ref[:, PB:] = tile(2) if pair else got_ref[mine]
+
+        @pl.when(role != 0)
+        def _():
+            if pair:
+                pan_ref[...] = got_ref[mine]
+            else:
+                pan_ref[:, :PB] = got_ref[mine]
+                pan_ref[:, PB:] = tile(1)
+
+        one = lax.dot_general(
+            pan_ref[:, :PB], one_ref[...], LAST_LAST, preferred_element_type=F32
+        ).astype(BF16)
+        partial = (
+            pan_ref[:, PB:].astype(F32)
+            - lax.dot_general(one, cross_ref[...], LAST_LAST, preferred_element_type=F32)
+        ).astype(BF16)
+        two = lax.dot_general(
+            partial, two_ref[...], LAST_LAST, preferred_element_type=F32
+        ).astype(BF16)
+        bas_ref[:, :PB] = one
+        bas_ref[:, PB:] = two
+        out_ref[...] = (
+            z_ref[...].astype(F32)
+            - lax.dot_general(
+                bas_ref[...], f_ref[...], LAST_LAST, preferred_element_type=F32
+            )
+        ).astype(BF16)
+
+        @pl.when(step // (lines // 2) == t[3])
+        def _():
+            half_ref[...] = bas_ref[...]
+
+    small = pl.BlockSpec((PB, PB), lambda j, t: (0, 0))
+    line = pl.BlockSpec((NY, width), lambda j, t: (j, 0))
+    last = lines // 2 - 1
+    return pl.pallas_call(
+        body,
+        grid_spec=pltpu.PrefetchScalarGridSpec(
+            num_scalar_prefetch=1,
+            grid=(lines,),
+            in_specs=[pl.BlockSpec(memory_space=pl.ANY)] * len(arrays)
+            + [line, small, small, small, pl.BlockSpec((width, 2 * PB), lambda j, t: (0, 0))],
+            out_specs=[
+                line,
+                pl.BlockSpec(
+                    (NY, 2 * PB), lambda j, t: (jnp.clip(j - t[3] * (last + 1), 0, last), 0)
+                ),
+            ],
+            scratch_shapes=[
+                pltpu.VMEM((lines, NY, block), BF16),
+                pltpu.VMEM((NY, 2 * PB), BF16),
+                pltpu.VMEM((NY, 2 * PB), BF16),
+                pltpu.SemaphoreType.DMA((lines,)),
+            ],
+        ),
+        out_shape=[
+            jax.ShapeDtypeStruct((cells, width), BF16),
+            jax.ShapeDtypeStruct((cells // 2, 2 * PB), BF16),
+        ],
+        compiler_params=pltpu.CompilerParams(vmem_limit_bytes=VMEM_BYTES),
+        cost_estimate=LITTLE,
+        name="finish",
+    )(info, *arrays, zfield, *solves, factor)
+
+
+def swap(value):
+    return lax.ppermute(value, "cols", SWAP)
+
+
+def bit_of(bit):
+    return lax.axis_index("rows") // bit % 2
+
+
+def row_bits():
+    count = lax.axis_size("rows")
+    return [1 << k for k in range(count.bit_length() - 1)]
+
+
+def over_rows(value, bit):
+    count = lax.axis_size("rows")
+    return lax.ppermute(value, "rows", [(k, k ^ bit) for k in range(count)])
+
+
+def sum_rows(value):
+    for bit in row_bits():
+        value = value + over_rows(value, bit)
+    return value
+
+
+def reduce_rows(split, whole=None):
+    for bit in row_bits():
+        half = split.shape[0] // 2
+        side = bit_of(bit)
+        keep = lax.dynamic_slice_in_dim(split, side * half, half, 0)
+        send = lax.dynamic_slice_in_dim(split, (1 - side) * half, half, 0)
+        if whole is None:
+            split = keep + over_rows(send, bit)
+        else:
+            got = over_rows(jnp.concatenate([send, whole], 0), bit)
+            split = keep + got[:half]
+            whole = whole + got[half:]
+    return split, whole
+
+
+def slice_start(width):
+    start = 0
+    for bit in row_bits():
+        width //= 2
+        start = start + bit_of(bit) * width
+    return start
+
+
+def gather_rows(value):
+    for bit in reversed(row_bits()):
+        other = over_rows(value, bit)
+        value = jnp.where(
+            bit_of(bit) == 0,
+            jnp.concatenate([value, other], 0),
+            jnp.concatenate([other, value], 0),
+        )
+    return value
+
+
+def dot_t(left, right):
+    return lax.dot_general(left, right, LAST_LAST, precision=HIGHEST, preferred_element_type=F32)
+
+
+def step_of(live, work, *values):
+    shapes = jax.eval_shape(work, *values)
+    empty = lambda *_: jax.tree.map(lambda shape: jnp.zeros(shape.shape, shape.dtype), shapes)
+    return lax.cond(live, work, empty, *values)
+
+
+def after(value, *events):
+    return lax.optimization_barrier((value, *events))[0]
+
+
+def two_groups(sketch, stiffness, reaction, panel_order):
+    cells, width = sketch.shape
+    lines = cells // NY
+    panels_here = width // PB
+    row_count = lax.axis_size("rows")
+    scale = 1.0 / (cells * row_count)
+    group = lax.axis_index("cols")
+    first, second = panel_order[0], panel_order[1]
+    group_one, group_two = first // panels_here, second // panels_here
+    share = width // row_count
+    eye = jnp.eye(PB, dtype=F32)
+    tile_one = first % panels_here
+    tile_two = second % panels_here
+    holds_one = group == group_one
+    role = jnp.where(holds_one, 0, 1)
+
+    def upward(value):
+        return lax.ppermute(value, "rows", [(i, i + 1) for i in range(row_count - 1)])
+
+    def downward(value):
+        return lax.ppermute(value, "rows", [(i + 1, i) for i in range(row_count - 1)])
+
+    def identity_rows(panel):
+        position = group * width + slice_start(width) + jnp.arange(share, dtype=jnp.int32)
+        offset = jnp.arange(PB, dtype=jnp.int32)
+        return (position[:, None] == panel * PB + offset[None, :]).astype(F32)
+
+    def factor_of(one, two, inverse_one, cross, inverse_two):
+        core_one = one * scale + identity_rows(first)
+        core_two = two * scale + identity_rows(second)
+        column_one = dot_t(core_one, inverse_one)
+        column_two = dot_t(core_two - dot_t(column_one, cross), inverse_two)
+        return gather_rows(jnp.concatenate([column_one, column_two], 1))
+
+    def apart(sketch, mix, stiff, info):
+        def order(slot, turned):
+            turned = jnp.asarray(turned, jnp.int32)
+            near = (slot + 1) & 3
+            return jnp.where((slot < 4) == (turned == 0), near, (slot & 3) + 4)
+
+        def sent(slot):
+            return lambda j, t: order(slot + j, t[0])
+
+        def came(slot):
+            return lambda j, t: order(slot + j, 1 - t[0])
+
+        own_tile = lambda j, t: t[1]
+        tile_after = lambda j, t: (t[1] + 1 + j) % panels_here
+        bottom, top = lambda j, t: lines - 1, lambda j, t: 0
+        early = panel_lines(sketch, mix, stiff, info, 3, sent(0), own_tile)
+        got_early = swap(early)
+        others = panels_here - 1
+
+        def own_halo(sketch, info):
+            low = upward(copy_lines(sketch, info, 1, bottom, own_tile))
+            return low, downward(copy_lines(sketch, info, 1, top, own_tile))
+
+        live = info[3] >= 0
+        low_own, high_own = step_of(live, own_halo, after(sketch, early), info)
+        late = panel_lines(sketch, mix, stiff, info, 3, sent(4), own_tile)
+        edges = panel_lines(
+            sketch,
+            mix,
+            stiff,
+            info,
+            2,
+            lambda j, t: order(3 + 4 * j, t[0]),
+            own_tile,
+            low_own,
+            high_own,
+        )
+        edge, last = edges[:, :PB], edges[:, PB:]
+        got_edge = swap(edge)
+        got_late = swap(after(late, edge))
+        got_last = swap(after(last, late, edge))
+
+        def halo_copies(own, rest):
+            copies = [(own, 0, 0, PB, lambda t: t[1] * PB)]
+            for j in range(others):
+                copies.append((rest, 0, j * PB, PB, lambda t, j=j: tile_after(j, t) * PB))
+            return copies
+
+        def local_field(sketch, mix, stiff, info, low_own, high_own):
+            low_rest = upward(copy_lines(sketch, info, others, bottom, tile_after))
+            high_rest = downward(copy_lines(sketch, info, others, top, tile_after))
+            low, high = halo_copies(low_own, low_rest), halo_copies(high_own, high_rest)
+            return whole_field(sketch, mix, stiff, info, 1, low, high)
+
+        zfield, own = step_of(
+            live, local_field, after(sketch, late, edges), mix, stiff, info, low_own, high_own
+        )
+        side = lambda j, t: (0, j)
+        half_one = gram_lines(
+            zfield, [(got_early, PB, side)], info, 3, came(0)
+        ) + gram_lines(zfield, [(got_edge, PB, side)], info, 1, came(3))
+
+        def first_sums(own, half_one, info):
+            own_rows = lambda value: lax.dynamic_slice_in_dim(value, info[1] * PB, PB, 0)
+            own_share, whole = reduce_rows(
+                own, jnp.concatenate([own_rows(own), own_rows(half_one)], 0)
+            )
+            return own_share, whole, inverse_factor(whole[:PB] * scale + eye)
+
+        own_share, whole, inverse_own = step_of(live, first_sums, own, half_one, info)
+        diag_own, mixed_own = whole[:PB], whole[PB:]
+        small = jnp.concatenate([jnp.where(holds_one, inverse_own, diag_own), mixed_own], 0)
+        got_small = swap(small)
+        half_two = gram_lines(zfield, [(after(got_late, whole), PB, side)], info, 3, came(4))
+        mixed_other = got_small[PB:]
+        inverse_one = jnp.where(holds_one, inverse_own, got_small[:PB])
+        diag_two = jnp.where(holds_one, got_small[:PB], diag_own)
+        mixed = jnp.where(holds_one, mixed_own.T + mixed_other, mixed_own + mixed_other.T)
+        rest = gram_lines(zfield, [(after(got_last, whole), PB, side)], info, 1, came(7))
+
+        def last_sums(other, own_share, inverse_one, diag_two, mixed):
+            cross = dot_t(mixed * scale, inverse_one)
+            inverse_two = inverse_factor(diag_two * scale + eye - dot_t(cross, cross))
+            other_share, _ = reduce_rows(other)
+            one = jnp.where(holds_one, own_share, other_share)
+            two = jnp.where(holds_one, other_share, own_share)
+            factor = factor_of(one, two, inverse_one, cross, inverse_two)
+            return factor, cross, inverse_two
+
+        factor, cross, inverse_two = step_of(
+            live,
+            last_sums,
+            (half_one + half_two) + rest,
+            own_share,
+            inverse_one,
+            diag_two,
+            mixed,
+        )
+
+        def slot_of(line, t):
+            near = (line + 3) & 3
+            return jnp.where(
+                t[0] == 0, jnp.where(line < 4, near + 4, line - 4), jnp.where(line < 4, near, line)
+            )
+
+        solves = [value.astype(BF16) for value in (inverse_one, cross, inverse_two)]
+        chunks = [(got_early, 0), (got_early, PB), (got_early, 2 * PB), (got_edge, 0)]
+        chunks += [(got_late, 0), (got_late, PB), (got_late, 2 * PB), (got_last, 0)]
+        residual, basis_rows = finish(
+            zfield, chunks, solves, factor.astype(BF16), info, False, slot_of
+        )
+        return residual, basis_rows, factor
+
+    def together(sketch, mix, stiff, info):
+        owner = holds_one
+        pairs = [(1, 2), (3, 4), (0, 7), (5, 6)]
+
+        def tile_at(j, t):
+            return jnp.where(j % 2 == 0, t[1], t[2])
+
+        def chunk(near, far):
+            return panel_lines(
+                sketch,
+                mix,
+                stiff,
+                info,
+                4,
+                lambda j, t: jnp.where(t[0] == 0, near + j // 2, far),
+                lambda j, t: jnp.where(t[0] == 0, tile_at(j, t), j),
+            )
+
+        chunk_one = chunk(1, 5)
+        got_one = swap(chunk_one)
+        chunk_two = chunk(3, 6)
+        got_two = swap(chunk_two)
+        live = info[3] >= 0
+        nothing = lambda j, t: 0
+        whole_line = lambda halo: [(halo, 0, 0, width, lambda t: 0)]
+
+        def local_field(sketch, mix, stiff, info):
+            low = upward(copy_lines(sketch, info, 1, lambda j, t: lines - 1, nothing, width))
+            high = downward(copy_lines(sketch, info, 1, nothing, nothing, width))
+            zfield, own = whole_field(
+                sketch, mix, stiff, info, 2, whole_line(low), whole_line(high)
+            )
+            chunks = [copy_lines(zfield, info, 4, lambda j, t: j // 2 * 7, tile_at)]
+            for line in (5, 6):
+                chunks.append(copy_lines(zfield, info, 2, lambda j, t, k=line: k, tile_at))
+            return zfield, own, *chunks
+
+        sketch = after(sketch, chunk_one, chunk_two)
+        zfield, own, chunk_three, chunk_four, chunk_five = step_of(
+            live, local_field, sketch, mix, stiff, info
+        )
+        got_three = swap(chunk_three)
+        got_four = swap(after(chunk_four, chunk_three))
+
+        def own_sums(own, info):
+            own_share, _ = reduce_rows(own)
+            total = gather_rows(own_share)
+            whole = jnp.concatenate(
+                [lax.dynamic_slice_in_dim(total, info[k] * PB, PB, 0) for k in (1, 2)], 0
+            )
+            inverse_one = inverse_factor(whole[:PB, :PB] * scale + eye)
+            cross = dot_t(whole[PB:, :PB] * scale, inverse_one)
+            schur = whole[PB:, PB:] * scale + eye - dot_t(cross, cross)
+            return own_share, inverse_one, cross, inverse_factor(schur)
+
+        own_share, inverse_one, cross, inverse_two = step_of(
+            live, own_sums, after(own, chunk_three), info
+        )
+
+        def owner_part(received, line):
+            return gram_lines(
+                received,
+                [
+                    (zfield, PB, lambda j, t: (line, t[1])),
+                    (zfield, PB, lambda j, t: (line, t[2])),
+                ],
+                info,
+                1,
+                lambda j, t: 0,
+            )
+
+        def other_part(received, pair):
+            return gram_lines(
+                zfield,
+                [(received, 2 * PB, lambda j, t: (0, j))],
+                info,
+                2,
+                lambda j, t: pair[0] + j * (pair[1] - pair[0]),
+            )
+
+        late_two = after(got_two, inverse_two)
+        owner_share = step_of(
+            live,
+            lambda part: reduce_rows(part)[0],
+            owner_part(got_one, 5) + owner_part(late_two, 6),
+        )
+        small = jnp.concatenate(
+            [inverse_one, cross, inverse_two, owner_share[:, :PB], owner_share[:, PB:]], 0
+        )
+        got_small = swap(small)
+        got_five = swap(after(chunk_five, got_small))
+        late_three = after(got_three, small)
+        inverse_one = jnp.where(owner, inverse_one, got_small[:PB])
+        cross = jnp.where(owner, cross, got_small[PB : 2 * PB])
+        inverse_two = jnp.where(owner, inverse_two, got_small[2 * PB : 3 * PB])
+        extra = jnp.concatenate(
+            [got_small[3 * PB : 3 * PB + share], got_small[3 * PB + share :]], 1
+        )
+        other_sum = (other_part(got_one, pairs[0]) + other_part(late_two, pairs[1])) + other_part(
+            late_three, pairs[2]
+        )
+
+        def last_sums(other_sum, own_share, extra, inverse_one, cross, inverse_two):
+            other_share, _ = reduce_rows(other_sum)
+            mine = jnp.where(owner, own_share, other_share + extra)
+            return factor_of(mine[:, :PB], mine[:, PB:], inverse_one, cross, inverse_two)
+
+        factor = step_of(
+            live, last_sums, other_sum, own_share, extra, inverse_one, cross, inverse_two
+        )
+
+        def slot_of(line, t):
+            return jnp.where(line == 0, 4, jnp.where(line == 7, 5, jnp.where(line < 5, line - 1, line + 1)))
+
+        solves = [value.astype(BF16) for value in (inverse_one, cross, inverse_two)]
+        chunks = [
+            (array, column) for array in (got_one, got_two, got_three) for column in (0, 2 * PB)
+        ]
+        chunks += [(got_four, 0), (after(got_five, factor), 0)]
+        residual, basis_rows = finish(
+            zfield, chunks, solves, factor.astype(BF16), info, True, slot_of
+        )
+        return residual, basis_rows, factor
+
+    stiff = stiffness.reshape(-1, LANES)
+    mix = (reaction + 4.0 * stiffness).reshape(-1, LANES)
+    same = group_one == group_two
+    info = jnp.stack(
+        [
+            role,
+            jnp.where(same | holds_one, tile_one, tile_two),
+            jnp.where(same | (role == 1), tile_two, tile_one),
+            group,
+        ]
+    ).astype(jnp.int32)
+    return lax.cond(same, together, apart, sketch, mix, stiff, info)
+
+
+def per_device(sketch, stiffness, reaction, panel_order):
+    cells, width = sketch.shape
+    rows = lax.axis_size("rows")
+    fits = lax.axis_size("cols") == 2 and cells == 8 * NY and width == 4 * PB
+    if fits and rows & (rows - 1) == 0 and rows > 1:
+        return two_groups(sketch, stiffness, reaction, panel_order)
+    return any_groups(sketch, stiffness, reaction, panel_order)
 
 
 def solution(mesh):

time: 547 us -> 227 us (0.41)
  waiting for transfers between devices: 352 us -> 43.7 us
  Pallas kernels: 0 us -> 112 us
  other arithmetic: 92.2 us -> 7.78 us
  matrix products: 47.1 us -> 2.71 us
  starting transfers between devices: 5.28 us -> 42.8 us
  local copies, waits for them, and re-layouts: 30.1 us -> 7.33 us
  between operations: 20.2 us -> 6.15 us
    psum x2 -> x0, waiting for transfers between devices: 330 us -> none  [the longest x1 240 us: spread(): return lax.psum(kept, axis)]
    pallas_call x0 -> x16, Pallas kernels: none -> 112 us  [the longest x2 25.6 us: field_part(): pl.pallas_call(body, grid_spec=pltpu.PrefetchScalarGridSpec(num_scalar_pr...]
    another operation x10 -> x1, other arithmetic: 45.9 us -> 0.08 us  [two_groups(): jnp.stack([role, jnp.where(same | holds_one, tile_one, tile_two), jnp.whe...]
    dot_general x7 -> x5, matrix products: 46.5 us -> 2.71 us  [dot_t(): lax.dot_general(left, right, LAST_LAST, precision=HIGHEST, preferred_elem...]
    ppermute x2 -> x21, waiting for transfers between devices: 0.01 us -> 43.7 us  [the longest x12 34.3 us: over_rows(): return lax.ppermute(value, 'rows', [(k, k ^ bit) for k in range(count)])]
    ppermute x2 -> x21, starting transfers between devices: 4.97 us -> 42.8 us  [the longest x12 21.9 us: over_rows(): return lax.ppermute(value, 'rows', [(k, k ^ bit) for k in range(count)])]
    convert_element_type x1 -> x4, other arithmetic: 36.1 us -> 2.36 us  [the longest x2 1.49 us: apart(): solves = [value.astype(BF16) for value in (inverse_one, cross, inverse_two)]]
    all_gather x1 -> x0, waiting for transfers between devices: 21.9 us -> none  [per_device(): gram_full = lax.all_gather(summed, 'cols', axis=0, tiled=True)]
  transfers between devices with their start and end apart: 5 -> 21, of which waited for: 3 -> 12; matrix products, arithmetic and copies ran while one was open for 2% -> 4% of each run, Pallas kernels for 0% -> 38%
where the time goes in v1:
time: 227 us; the launch traced here: 225 us
  Pallas kernels  112 us (49%)
  waiting for transfers between devices  43.7 us (19%)
  starting transfers between devices  42.8 us (19%)
  other arithmetic  7.78 us (3%)
  local copies, waits for them, and re-layouts  7.33 us (3%)
  between operations  6.15 us (3%)
  matrix products  2.71 us (1%)
  loops' own time  2.49 us (1%)
    ppermute x12, waiting for transfers between devices, over_rows(): return lax.ppermute(value, 'rows', [(k, k ^ bit) for k in range(count)])  34.3 us
    pallas_call x2, Pallas kernels, field_part(): pl.pallas_call(body, grid_spec=pltpu.PrefetchScalarGridSpec(num_scalar_pr...  25.6 us
    ppermute x12, starting transfers between devices, over_rows(): return lax.ppermute(value, 'rows', [(k, k ^ bit) for k in range(count)])  21.9 us
    pallas_call x1, Pallas kernels, finish(): pl.pallas_call(body, grid_spec=pltpu.PrefetchScalarGridSpec(num_scalar_pr...  21.8 us
    pallas_call x2, Pallas kernels, inverse_factor(): pl.pallas_call(body, out_shape=jax.ShapeDtypeStruct((PB, PB), F32), scrat...  18.7 us
    pallas_call x4, Pallas kernels, gram_lines(): pl.pallas_call(body, grid_spec=pltpu.PrefetchScalarGridSpec(num_scalar_pr...  17.4 us
    pallas_call x3, Pallas kernels, panel_lines(): pl.pallas_call(body, grid_spec=pltpu.PrefetchScalarGridSpec(num_scalar_pr...  16 us
    pallas_call x4, Pallas kernels, copy_lines(): pl.pallas_call(body, grid_spec=pltpu.PrefetchScalarGridSpec(num_scalar_pr...  12.8 us
  transfers between devices with their start and end apart: 21, of which 12 were waited for; matrix products, arithmetic and copies ran while one was open for 4% of the time, Pallas kernels for 38%

profile of v1, /device:TPU:0, one launch (start us, length us, event | category | flops | bytes accessed | tf_op | source)
XLA Modules:
  0.0 225.4 jit_solution(6124312895676504380)
XLA Ops:
  0.6 1.3 fusion.59
  7.3 0.9 add_bitcast_fusion
  8.2 217.0 %conditional.9 = (bf16[16384,512]{1,0:T(8,128)(2,1)}, bf16[8192,256]{1,0:T(8,128)(2,1)}, f32[512,256]{1,0:T(8,128)}) conditional(s32[]{:T(128)} %convert_element_type.60, (s32[4]{0:T(128)S(1)}, bf16[16384,512]{1,0:T(8,128)(2,1)}, f32[128,128]{1,0:T(8,128)S(1)}, f32[128,128]{1,0:T(8,128)}, s32[]{:T(128)}, /*index=5*/pred[]{:T(512)}, s32[]{:T(128)}, ...), branch_computations={%region_0.9_spmd, %region_9.18_spmd} | conditional | flops 89830024 | bytes 115155192 | solution.py:909
  8.2 5.7 %panel_lines.5 = bf16[2048,384]{1,0:T(8,128)(2,1)} custom-call(s32[4]{0:T(128)S(1)} %get-tuple-element.200.info_ref.t, bf16[16384,512]{1,0:T(8,128)(2,1)} %get-tuple-element.210.up_ref.mid_ref.down_ref, bf16[16384,512]{1,0:T(8,128)(2,1)} %get-tuple-element.210.up_ref.mid_ref.down_ref, bf16[16384,512]{1,0:T(8,128)(2,1)} %get-tuple-element.210.up_ref.mid_ref.down_ref, ...), custom_call_target="tpu_custom_call" | custom-call | flops 1048576 | bytes 16384 | tf_op jit(solution)/shard_map/cond/branch_0_fun/panel_lines/pallas_call | solution.py:189
  13.9 2.9 %collective-permute-start.22 = (bf16[2048,384]{1,0:T(8,128)(2,1)}, bf16[2048,384]{1,0:T(8,128)(2,1)S(1)}, u32[]{:S(2)}, u32[]{:S(2)}) collective-permute-start(bf16[2048,384]{1,0:T(8,128)(2,1)} %panel_lines.5), channel_id=1, source_target_pairs={{0,1},{1,0},{2,3},{3,2},{4,5},{5,4},{6,7},{7,6},{8,9},{9,8},{10,11... | collective-permute-start | bytes 4718600 | tf_op jit(solution)/shard_map/cond/branch_0_fun/ppermute | solution.py:556
  16.9 5.7 %panel_lines.7 = bf16[2048,384]{1,0:T(8,128)(2,1)} custom-call(s32[4]{0:T(128)S(1)} %get-tuple-element.200.info_ref.t, bf16[16384,512]{1,0:T(8,128)(2,1)} %get-tuple-element.210.up_ref.mid_ref.down_ref, bf16[16384,512]{1,0:T(8,128)(2,1)} %get-tuple-element.210.up_ref.mid_ref.down_ref, bf16[16384,512]{1,0:T(8,128)(2,1)} %get-tuple-element.210.up_ref.mid_ref.down_ref, ...), custom_call_target="tpu_custom_call" | custom-call | flops 1048576 | bytes 16384 | tf_op jit(solution)/shard_map/cond/branch_0_fun/panel_lines/pallas_call | solution.py:189
  22.5 12.0 %conditional = (bf16[2048,128]{1,0:T(8,128)(2,1)}, bf16[2048,128]{1,0:T(8,128)(2,1)}) conditional(s32[]{:T(128)} %convert_element_type.46, () %tuple.63, (s32[4]{0:T(128)S(1)}, bf16[16384,512]{1,0:T(8,128)(2,1)}) %tuple.65), branch_computations={%region_1.1_spmd, %region_2.2_spmd} | conditional | flops 2097152 | bytes 4227168 | solution.py:620
  22.5 2.4 %copy_lines.9 = bf16[2048,128]{1,0:T(8,128)(2,1)} custom-call(s32[4]{0:T(128)S(1)} %get-tuple-element.167.info_ref, bf16[16384,512]{1,0:T(8,128)(2,1)} %get-tuple-element.168.z_ref), custom_call_target="tpu_custom_call" | custom-call | flops 1048576 | bytes 16384 | tf_op jit(solution)/shard_map/cond/branch_0_fun/cond/branch_1_fun/copy_lines/pallas_call | solution.py:352
  24.9 2.3 %collective-permute-start = (bf16[2048,128]{1,0:T(8,128)(2,1)}, bf16[2048,128]{1,0:T(8,128)(2,1)}, u32[]{:S(2)}, u32[]{:S(2)}) collective-permute-start(bf16[2048,128]{1,0:T(8,128)(2,1)} %copy_lines.9), channel_id=1, source_target_pairs={{0,2},{2,4},{4,6},{6,8},{8,10},{10,12},{12,14},{14,16},{16,18},{18... | collective-permute-start | bytes 1572872 | tf_op jit(solution)/shard_map/cond/branch_0_fun/cond/branch_1_fun/ppermute | solution.py:644
  27.2 2.4 %copy_lines.10 = bf16[2048,128]{1,0:T(8,128)(2,1)} custom-call(s32[4]{0:T(128)S(1)} %get-tuple-element.167.info_ref, bf16[16384,512]{1,0:T(8,128)(2,1)} %get-tuple-element.168.z_ref), custom_call_target="tpu_custom_call" | custom-call | flops 1048576 | bytes 16384 | tf_op jit(solution)/shard_map/cond/branch_0_fun/cond/branch_1_fun/copy_lines/pallas_call | solution.py:352
  29.6 1.3 collective-permute-start.1
  30.9 3.6 %collective-permute-done.1 = bf16[2048,128]{1,0:T(8,128)(2,1)} collective-permute-done((bf16[2048,128]{1,0:T(8,128)(2,1)}, bf16[2048,128]{1,0:T(8,128)(2,1)}, u32[]{:S(2)}, u32[]{:S(2)}) %collective-permute-start.1) | collective-permute-done | bytes 524320 | tf_op jit(solution)/shard_map/cond/branch_0_fun/cond/branch_1_fun/ppermute | solution.py:647
  34.5 4.7 %panel_lines.6 = bf16[2048,256]{1,0:T(8,128)(2,1)} custom-call(s32[4]{0:T(128)S(1)} %get-tuple-element.200.info_ref.t, bf16[16384,512]{1,0:T(8,128)(2,1)} %get-tuple-element.210.up_ref.mid_ref.down_ref, bf16[16384,512]{1,0:T(8,128)(2,1)} %get-tuple-element.210.up_ref.mid_ref.down_ref, bf16[16384,512]{1,0:T(8,128)(2,1)} %get-tuple-element.210.up_ref.mid_ref.down_ref, ...), custom_call_target="tpu_custom_call" | custom-call | flops 1048576 | bytes 16384 | tf_op jit(solution)/shard_map/cond/branch_0_fun/panel_lines/pallas_call | solution.py:189
  39.2 2.1 fusion.57
  41.8 1.5 collective-permute-start.23
  43.3 46.6 %conditional.1 = (bf16[16384,512]{1,0:T(8,128)(2,1)}, f32[512,128]{1,0:T(8,128)S(1)}) conditional(s32[]{:T(128)} %convert_element_type.46, () %tuple.68, (s32[4]{0:T(128)S(1)}, bf16[16384,512]{1,0:T(8,128)(2,1)}, f32[128,128]{1,0:T(8,128)S(1)}, f32[128,128]{1,0:T(8,128)S(1)}, bf16[2048,128]{1,0:T(8,128)(2,1)}, ...), branch_computations={%region_3.3_spmd, %region_4.4_spmd} | conditional | flops 4259840 | bytes 27066548 | solution.py:620
  43.3 4.0 %copy_lines.11 = bf16[2048,384]{1,0:T(8,128)(2,1)} custom-call(s32[4]{0:T(128)S(1)} %get-tuple-element.169.info_ref, bf16[16384,512]{1,0:T(8,128)(2,1)} %get-tuple-element.171.z_ref.refs_0_.refs_2_), custom_call_target="tpu_custom_call" | custom-call | flops 1048576 | bytes 16384 | tf_op jit(solution)/shard_map/cond/branch_0_fun/cond/branch_1_fun/copy_lines/pallas_call | solution.py:352
  47.3 8.8 %collective-permute-start.2 = (bf16[2048,384]{1,0:T(8,128)(2,1)}, bf16[2048,384]{1,0:T(8,128)(2,1)S(1)}, u32[]{:S(2)}, u32[]{:S(2)}) collective-permute-start(bf16[2048,384]{1,0:T(8,128)(2,1)} %copy_lines.11), channel_id=1, source_target_pairs={{0,2},{2,4},{4,6},{6,8},{8,10},{10,12},{12,14},{14,16},{16,18},{18... | collective-permute-start | bytes 4718600 | tf_op jit(solution)/shard_map/cond/branch_0_fun/cond/branch_1_fun/ppermute | solution.py:644
  56.1 4.0 %copy_lines.12 = bf16[2048,384]{1,0:T(8,128)(2,1)} custom-call(s32[4]{0:T(128)S(1)} %get-tuple-element.169.info_ref, bf16[16384,512]{1,0:T(8,128)(2,1)} %get-tuple-element.171.z_ref.refs_0_.refs_2_), custom_call_target="tpu_custom_call" | custom-call | flops 1048576 | bytes 16384 | tf_op jit(solution)/shard_map/cond/branch_0_fun/cond/branch_1_fun/copy_lines/pallas_call | solution.py:352
  60.1 1.5 collective-permute-start.3
  61.6 16.7 %field_part.4 = (bf16[16384,512]{1,0:T(8,128)(2,1)}, f32[512,128]{1,0:T(8,128)}) custom-call(s32[4]{0:T(128)S(1)} %get-tuple-element.169.info_ref, bf16[16384,512]{1,0:T(8,128)(2,1)} %get-tuple-element.171.z_ref.refs_0_.refs_2_, f32[128,128]{1,0:T(8,128)S(1)} %get-tuple-element.173.refs_1_.refs_5_, f32[128,128]{1,0:T(8,128)S(1)} %get-tuple-element.174.refs_2_.refs_6_), custom_call_target="tpu_custom_call" | custom-call | flops 1048576 | bytes 16384 | tf_op jit(solution)/shard_map/cond/branch_0_fun/cond/branch_1_fun/field_part/pallas_call | solution.py:288
  78.3 1.1 copy-done.8
  80.0 9.0 %field_part.5 = (bf16[16384,512]{1,0:T(8,128)(2,1)}, f32[512,128]{1,0:T(8,128)}) custom-call(s32[4]{0:T(128)S(1)} %get-tuple-element.169.info_ref, bf16[2048,128]{1,0:T(8,128)(2,1)} %get-tuple-element.170.refs_0_, bf16[2048,384]{1,0:T(8,128)(2,1)} %copy-done.8, ...), custom_call_target="tpu_custom_call", output_to_operand_aliasing={{0}: (8, {})} | custom-call | flops 1048576 | bytes 16384 | tf_op jit(solution)/shard_map/cond/branch_0_fun/cond/branch_1_fun/field_part/pallas_call | solution.py:288
  89.0 1.0 add.359
  89.9 0.6 collective-permute-start.25
  90.6 5.8 %collective-permute-done.23.rest_0_.refs_1_ = bf16[2048,128]{1,0:T(8,128)(2,1)S(1)} collective-permute-done((bf16[2048,128]{1,0:T(8,128)(2,1)}, bf16[2048,128]{1,0:T(8,128)(2,1)S(1)}, u32[]{:S(2)}, u32[]{:S(2)}) %collective-permute-start.23) | collective-permute-done | bytes 524320 | tf_op jit(solution)/shard_map/cond/branch_0_fun/ppermute | solution.py:556
  96.4 0.8 copy-done.6
  97.2 3.6 %gram_lines.10 = f32[512,128]{1,0:T(8,128)} custom-call(s32[4]{0:T(128)S(1)} %get-tuple-element.200.info_ref.t, bf16[16384,512]{1,0:T(8,128)(2,1)} %get-tuple-element.211.z_ref.refs_4_, bf16[2048,128]{1,0:T(8,128)(2,1)} %copy-done.6), custom_call_target="tpu_custom_call" | custom-call | flops 1048576 | bytes 16384 | tf_op jit(solution)/shard_map/cond/branch_0_fun/gram_lines/pallas_call | solution.py:390
  100.8 1.2 copy-done.3
  101.9 5.8 %gram_lines.9 = f32[512,128]{1,0:T(8,128)} custom-call(s32[4]{0:T(128)S(1)} %get-tuple-element.200.info_ref.t, bf16[16384,512]{1,0:T(8,128)(2,1)} %get-tuple-element.211.z_ref.refs_4_, bf16[2048,384]{1,0:T(8,128)(2,1)} %copy-done.3), custom_call_target="tpu_custom_call" | custom-call | flops 1048576 | bytes 16384 | tf_op jit(solution)/shard_map/cond/branch_0_fun/gram_lines/pallas_call | solution.py:390
  107.7 1.0 add.415
  108.7 43.1 %conditional.2 = (f32[32,128]{1,0:T(8,128)S(1)}, f32[256,128]{1,0:T(8,128)}, f32[128,128]{1,0:T(8,128)S(1)}, f32[128,128]{1,0:T(8,128)S(1)}, f32[128,128]{1,0:T(8,128)S(1)}) conditional(s32[]{:T(128)} %convert_element_type.46, () %tuple.71, (f32[512,128]{1,0:T(8,128)S(1)}, s32[]{:T(128)}, f32[512,128]{1,0:T(8,128)S(1)}, ...), branch_computations={%region_5.5_spmd, %region_6.6_spmd} | conditional | flops 1564787 | bytes 8095146 | solution.py:620
  108.8 6.5 %collective-permute-start.6 = (f32[512,128]{1,0:T(8,128)S(1)}, f32[512,128]{1,0:T(8,128)S(1)}, u32[]{:S(2)}, u32[]{:S(2)}) collective-permute-start(f32[512,128]{1,0:T(8,128)S(1)} %pad_maximum_fusion), channel_id=1, source_target_pairs={{0,2},{2,0},{4,6},{6,4},{8,10},{10,8},{12,14},{14,12},{16,18},{18,... | collective-permute-start | bytes 786440 | tf_op jit(solution)/shard_map/cond/branch_0_fun/cond/branch_1_fun/ppermute | solution.py:570
  115.3 1.2 collective-permute-done.6
  116.5 3.0 %collective-permute-start.7 = (f32[384,128]{1,0:T(8,128)S(1)}, f32[384,128]{1,0:T(8,128)S(1)}, u32[]{:S(2)}, u32[]{:S(2)}) collective-permute-start(f32[384,128]{1,0:T(8,128)S(1)} %pad_maximum_fusion.1), channel_id=1, source_target_pairs={{0,4},{2,6},{4,0},{6,2},{8,12},{10,14},{12,8},{14,10},{16,20},{18,... | collective-permute-start | bytes 589832 | tf_op jit(solution)/shard_map/cond/branch_0_fun/cond/branch_1_fun/ppermute | solution.py:570
  119.5 5.2 %collective-permute-done.7 = f32[384,128]{1,0:T(8,128)S(1)} collective-permute-done((f32[384,128]{1,0:T(8,128)S(1)}, f32[384,128]{1,0:T(8,128)S(1)}, u32[]{:S(2)}, u32[]{:S(2)}) %collective-permute-start.7) | collective-permute-done | bytes 196640 | tf_op jit(solution)/shard_map/cond/branch_0_fun/cond/branch_1_fun/ppermute | solution.py:570
  124.8 2.8 %collective-permute-start.8 = (f32[320,128]{1,0:T(8,128)S(1)}, f32[320,128]{1,0:T(8,128)S(1)}, u32[]{:S(2)}, u32[]{:S(2)}) collective-permute-start(f32[320,128]{1,0:T(8,128)S(1)} %pad_maximum_fusion.2), channel_id=1, source_target_pairs={{0,8},{2,10},{4,12},{6,14},{8,0},{10,2},{12,4},{14,6},{16,24},{18,... | collective-permute-start | bytes 491528 | tf_op jit(solution)/shard_map/cond/branch_0_fun/cond/branch_1_fun/ppermute | solution.py:570
  127.6 3.9 %collective-permute-done.8 = f32[320,128]{1,0:T(8,128)S(1)} collective-permute-done((f32[320,128]{1,0:T(8,128)S(1)}, f32[320,128]{1,0:T(8,128)S(1)}, u32[]{:S(2)}, u32[]{:S(2)}) %collective-permute-start.8) | collective-permute-done | bytes 163872 | tf_op jit(solution)/shard_map/cond/branch_0_fun/cond/branch_1_fun/ppermute | solution.py:570
  131.6 2.8 %collective-permute-start.9 = (f32[288,128]{1,0:T(8,128)S(1)}, f32[288,128]{1,0:T(8,128)S(1)}, u32[]{:S(2)}, u32[]{:S(2)}) collective-permute-start(f32[288,128]{1,0:T(8,128)S(1)} %pad_maximum_fusion.3), channel_id=1, source_target_pairs={{0,16},{2,18},{4,20},{6,22},{8,24},{10,26},{12,28},{14,30},{16,0},... | collective-permute-start | bytes 442376 | tf_op jit(solution)/shard_map/cond/branch_0_fun/cond/branch_1_fun/ppermute | solution.py:570
  134.4 6.0 %collective-permute-done.9 = f32[288,128]{1,0:T(8,128)S(1)} collective-permute-done((f32[288,128]{1,0:T(8,128)S(1)}, f32[288,128]{1,0:T(8,128)S(1)}, u32[]{:S(2)}, u32[]{:S(2)}) %collective-permute-start.9) | collective-permute-done | bytes 147488 | tf_op jit(solution)/shard_map/cond/branch_0_fun/cond/branch_1_fun/ppermute | solution.py:570
  140.4 0.7 slice_add_fusion
  141.1 1.5 multiply_add_fusion
  142.6 9.2 %inverse_factor.4 = f32[128,128]{1,0:T(8,128)S(1)} custom-call(f32[128,128]{1,0:T(8,128)} %get-tuple-element.313.a_ref), custom_call_target="tpu_custom_call" | custom-call | flops 1048576 | bytes 16384 | tf_op jit(solution)/shard_map/cond/branch_0_fun/cond/branch_1_fun/inverse_factor/pallas_call | solution.py:439
  151.9 1.6 collective-permute-start.26
  153.6 5.1 %gram_lines.11 = f32[512,128]{1,0:T(8,128)S(1)} custom-call(s32[4]{0:T(128)S(1)} %get-tuple-element.200.info_ref.t, bf16[16384,512]{1,0:T(8,128)(2,1)} %get-tuple-element.211.z_ref.refs_4_, bf16[2048,384]{1,0:T(8,128)(2,1)} %collective-permute-done.24.rest_0_.refs_2_), custom_call_target="tpu_custom_call" | custom-call | flops 1048576 | bytes 16384 | tf_op jit(solution)/shard_map/cond/branch_0_fun/gram_lines/pallas_call | solution.py:390
  158.7 2.9 %gram_lines.12 = f32[512,128]{1,0:T(8,128)S(1)} custom-call(s32[4]{0:T(128)S(1)} %get-tuple-element.200.info_ref.t, bf16[16384,512]{1,0:T(8,128)(2,1)} %get-tuple-element.211.z_ref.refs_4_, bf16[2048,128]{1,0:T(8,128)(2,1)} %copy-done.7), custom_call_target="tpu_custom_call" | custom-call | flops 1048576 | bytes 16384 | tf_op jit(solution)/shard_map/cond/branch_0_fun/gram_lines/pallas_call | solution.py:390
  161.6 0.6 fusion.50
  162.2 40.6 %conditional.3 = (f32[512,256]{1,0:T(8,128)}, bf16[512,256]{1,0:T(8,128)(2,1)S(1)}, bf16[128,128]{1,0:T(8,128)(2,1)S(1)}, bf16[128,128]{1,0:T(8,128)(2,1)S(1)}) conditional(s32[]{:T(128)} %convert_element_type.46, () %tuple.73, (pred[]{:T(512)}, f32[512,128]{1,0:T(8,128)S(1)}, f32[512,128]{1,0:T(8,128)S(1)}, f32[512,128]{1,0:T(8,128)S(1)}, ...), branch_computations={%region_7.7_spmd, %region_8.8_spmd} | conditional | flops 71569696 | bytes 8885022 | solution.py:620
  163.5 0.9 convolution_subtract_fusion.a_ref
  164.9 4.1 %collective-permute-done.15 = f32[128,128]{1,0:T(8,128)S(1)} collective-permute-done((f32[128,128]{1,0:T(8,128)S(1)}, f32[128,128]{1,0:T(8,128)S(1)}, u32[]{:S(2)}, u32[]{:S(2)}) %collective-permute-start.15) | collective-permute-done | bytes 65568 | tf_op jit(solution)/shard_map/cond/branch_0_fun/cond/branch_1_fun/ppermute | solution.py:570
  169.0 0.6 collective-permute-start.16
  170.3 2.7 %collective-permute-done.16 = f32[64,128]{1,0:T(8,128)S(1)} collective-permute-done((f32[64,128]{1,0:T(8,128)S(1)}, f32[64,128]{1,0:T(8,128)S(1)}, u32[]{:S(2)}, u32[]{:S(2)}) %collective-permute-start.16) | collective-permute-done | bytes 32800 | tf_op jit(solution)/shard_map/cond/branch_0_fun/cond/branch_1_fun/ppermute | solution.py:570
  173.0 1.9 collective-permute-start.17
  175.0 9.5 %inverse_factor.5 = f32[128,128]{1,0:T(8,128)} custom-call(f32[128,128]{1,0:T(8,128)} %convolution_subtract_fusion.a_ref), custom_call_target="tpu_custom_call" | custom-call | flops 1048576 | bytes 16384 | tf_op jit(solution)/shard_map/cond/branch_0_fun/cond/branch_1_fun/inverse_factor/pallas_call | solution.py:439
  184.9 1.1 fusion.6
  186.1 1.1 collective-permute-start.18
  187.2 3.8 %collective-permute-done.18 = f32[32,256]{1,0:T(8,128)S(1)} collective-permute-done((f32[32,256]{1,0:T(8,128)S(1)}, f32[32,256]{1,0:T(8,128)S(1)}, u32[]{:S(2)}, u32[]{:S(2)}) %collective-permute-start.18) | collective-permute-done | bytes 32800 | tf_op jit(solution)/shard_map/cond/branch_0_fun/cond/branch_1_fun/ppermute | solution.py:570
  191.0 2.1 collective-permute-start.19
  193.1 2.2 collective-permute-done.19
  195.8 4.5 %collective-permute-done.20 = f32[128,256]{1,0:T(8,128)S(1)} collective-permute-done((f32[128,256]{1,0:T(8,128)S(1)}, f32[128,256]{1,0:T(8,128)S(1)}, u32[]{:S(2)}, u32[]{:S(2)}) %collective-permute-start.20) | collective-permute-done | bytes 131104 | tf_op jit(solution)/shard_map/cond/branch_0_fun/cond/branch_1_fun/ppermute | solution.py:570
  200.5 0.8 convert_element_type.45
  201.3 0.7 collective-permute-done.21
  202.0 0.9 fusion.49
  202.8 21.8 %finish.2 = (bf16[16384,512]{1,0:T(8,128)(2,1)}, bf16[8192,256]{1,0:T(8,128)(2,1)}) custom-call(s32[4]{0:T(128)S(1)} %get-tuple-element.200.info_ref.t, bf16[2048,384]{1,0:T(8,128)(2,1)} %copy-done.3, bf16[2048,128]{1,0:T(8,128)(2,1)} %copy-done.6, bf16[2048,384]{1,0:T(8,128)(2,1)} %collective-permute-done.24.rest_0_.refs_2_, bf16[2048,128]{1,0:T(8,128)(2,1)} %copy-done.7, ...), custom_call_target="tpu_custom_call" | custom-call | flops 1048576 | bytes 16384 | tf_op jit(solution)/shard_map/cond/branch_0_fun/finish/pallas_call | solution.py:525
  (67 shorter events, 3.6 us)
Async XLA Ops:
  8.2 8.6 %copy-start.1 = (f32[128,128]{1,0:T(8,128)S(1)}, f32[128,128]{1,0:T(8,128)}, u32[]{:S(2)}) copy-start(f32[128,128]{1,0:T(8,128)} %get-tuple-element.203.stiff_ref) | copy-start | bytes 196612 | tf_op jit(solution)/shard_map/cond
  13.9 86.8 %collective-permute-start.22 = (bf16[2048,384]{1,0:T(8,128)(2,1)}, bf16[2048,384]{1,0:T(8,128)(2,1)S(1)}, u32[]{:S(2)}, u32[]{:S(2)}) collective-permute-start(bf16[2048,384]{1,0:T(8,128)(2,1)} %panel_lines.5), channel_id=1, source_target_pairs={{0,1},{1,0},{2,3},{3,2},{4,5},{5,4},{6,7},{7,6},{8,9},{9,8},{10,11... | collective-permute-start | bytes 4718600 | tf_op jit(solution)/shard_map/cond/branch_0_fun/ppermute | solution.py:556
  24.9 6.0 %collective-permute-start = (bf16[2048,128]{1,0:T(8,128)(2,1)}, bf16[2048,128]{1,0:T(8,128)(2,1)}, u32[]{:S(2)}, u32[]{:S(2)}) collective-permute-start(bf16[2048,128]{1,0:T(8,128)(2,1)} %copy_lines.9), channel_id=1, source_target_pairs={{0,2},{2,4},{4,6},{6,8},{8,10},{10,12},{12,14},{14,16},{16,18},{18... | collective-permute-start | bytes 1572872 | tf_op jit(solution)/shard_map/cond/branch_0_fun/cond/branch_1_fun/ppermute | solution.py:644
  29.6 4.9 %collective-permute-start.1 = (bf16[2048,128]{1,0:T(8,128)(2,1)}, bf16[2048,128]{1,0:T(8,128)(2,1)}, u32[]{:S(2)}, u32[]{:S(2)}) collective-permute-start(bf16[2048,128]{1,0:T(8,128)(2,1)} %copy_lines.10), channel_id=1, source_target_pairs={{2,0},{4,2},{6,4},{8,6},{10,8},{12,10},{14,12},{16,14},{18,16},{20... | collective-permute-start | bytes 1572872 | tf_op jit(solution)/shard_map/cond/branch_0_fun/cond/branch_1_fun/ppermute | solution.py:647
  41.3 112.3 %collective-permute-start.24 = (bf16[2048,384]{1,0:T(8,128)(2,1)}, bf16[2048,384]{1,0:T(8,128)(2,1)}, u32[]{:S(2)}, u32[]{:S(2)}) collective-permute-start(bf16[2048,384]{1,0:T(8,128)(2,1)} %panel_lines.7), channel_id=1, source_target_pairs={{0,1},{1,0},{2,3},{3,2},{4,5},{5,4},{6,7},{7,6},{8,9},{9,8},{10,11... | collective-permute-start | bytes 4718600 | tf_op jit(solution)/shard_map/cond/branch_0_fun/ppermute | solution.py:556
  41.8 54.5 %collective-permute-start.23 = (bf16[2048,128]{1,0:T(8,128)(2,1)}, bf16[2048,128]{1,0:T(8,128)(2,1)S(1)}, u32[]{:S(2)}, u32[]{:S(2)}) collective-permute-start(bf16[2048,128]{1,0:T(8,128)(2,1)} %get-tuple-element.337), channel_id=1, source_target_pairs={{0,1},{1,0},{2,3},{3,2},{4,5},{5,4},{6,7},{7,6},{8,9},{9,8},{10,11... | collective-permute-start | bytes 1572872 | tf_op jit(solution)/shard_map/cond/branch_0_fun/ppermute | solution.py:556
  47.3 31.0 %collective-permute-start.2 = (bf16[2048,384]{1,0:T(8,128)(2,1)}, bf16[2048,384]{1,0:T(8,128)(2,1)S(1)}, u32[]{:S(2)}, u32[]{:S(2)}) collective-permute-start(bf16[2048,384]{1,0:T(8,128)(2,1)} %copy_lines.11), channel_id=1, source_target_pairs={{0,2},{2,4},{4,6},{6,8},{8,10},{10,12},{12,14},{14,16},{16,18},{18... | collective-permute-start | bytes 4718600 | tf_op jit(solution)/shard_map/cond/branch_0_fun/cond/branch_1_fun/ppermute | solution.py:644
  60.1 18.2 %collective-permute-start.3 = (bf16[2048,384]{1,0:T(8,128)(2,1)}, bf16[2048,384]{1,0:T(8,128)(2,1)S(1)}, u32[]{:S(2)}, u32[]{:S(2)}) collective-permute-start(bf16[2048,384]{1,0:T(8,128)(2,1)} %copy_lines.12), channel_id=1, source_target_pairs={{2,0},{4,2},{6,4},{8,6},{10,8},{12,10},{14,12},{16,14},{18,16},{20... | collective-permute-start | bytes 4718600 | tf_op jit(solution)/shard_map/cond/branch_0_fun/cond/branch_1_fun/ppermute | solution.py:647
  78.3 1.2 copy-start.8
  78.3 1.7 copy-start.9
  80.0 9.0 %copy-start.14 = (f32[512,128]{1,0:T(8,128)S(1)}, f32[512,128]{1,0:T(8,128)}, u32[]{:S(2)}) copy-start(f32[512,128]{1,0:T(8,128)} %get-tuple-element.177) | copy-start | bytes 786436 | tf_op jit(solution)/shard_map/cond/branch_0_fun/cond
  89.9 63.6 %collective-permute-start.25 = (bf16[2048,128]{1,0:T(8,128)(2,1)S(1)}, bf16[2048,128]{1,0:T(8,128)(2,1)S(1)}, u32[]{:S(2)}, u32[]{:S(2)}) collective-permute-start(bf16[2048,128]{1,0:T(8,128)(2,1)S(1)} %get-tuple-element.209), channel_id=1, source_target_pairs={{0,1},{1,0},{2,3},{3,2},{4,5},{5,4},{6,7},{7,6},{8,9},{9,8},{10,11... | collective-permute-start | bytes 1572872 | tf_op jit(solution)/shard_map/cond/branch_0_fun/ppermute | solution.py:556
  96.4 0.8 copy-start.6
  100.7 7.0 %copy-start.10 = (f32[512,128]{1,0:T(8,128)S(1)}, f32[512,128]{1,0:T(8,128)}, u32[]{:S(2)}) copy-start(f32[512,128]{1,0:T(8,128)} %gram_lines.10) | copy-start | bytes 786436 | tf_op jit(solution)/shard_map/cond
  100.7 1.2 copy-start.3
  108.8 7.6 %collective-permute-start.6 = (f32[512,128]{1,0:T(8,128)S(1)}, f32[512,128]{1,0:T(8,128)S(1)}, u32[]{:S(2)}, u32[]{:S(2)}) collective-permute-start(f32[512,128]{1,0:T(8,128)S(1)} %pad_maximum_fusion), channel_id=1, source_target_pairs={{0,2},{2,0},{4,6},{6,4},{8,10},{10,8},{12,14},{14,12},{16,18},{18,... | collective-permute-start | bytes 786440 | tf_op jit(solution)/shard_map/cond/branch_0_fun/cond/branch_1_fun/ppermute | solution.py:570
  116.5 8.2 %collective-permute-start.7 = (f32[384,128]{1,0:T(8,128)S(1)}, f32[384,128]{1,0:T(8,128)S(1)}, u32[]{:S(2)}, u32[]{:S(2)}) collective-permute-start(f32[384,128]{1,0:T(8,128)S(1)} %pad_maximum_fusion.1), channel_id=1, source_target_pairs={{0,4},{2,6},{4,0},{6,2},{8,12},{10,14},{12,8},{14,10},{16,20},{18,... | collective-permute-start | bytes 589832 | tf_op jit(solution)/shard_map/cond/branch_0_fun/cond/branch_1_fun/ppermute | solution.py:570
  124.8 6.8 %collective-permute-start.8 = (f32[320,128]{1,0:T(8,128)S(1)}, f32[320,128]{1,0:T(8,128)S(1)}, u32[]{:S(2)}, u32[]{:S(2)}) collective-permute-start(f32[320,128]{1,0:T(8,128)S(1)} %pad_maximum_fusion.2), channel_id=1, source_target_pairs={{0,8},{2,10},{4,12},{6,14},{8,0},{10,2},{12,4},{14,6},{16,24},{18,... | collective-permute-start | bytes 491528 | tf_op jit(solution)/shard_map/cond/branch_0_fun/cond/branch_1_fun/ppermute | solution.py:570
  131.6 8.8 %collective-permute-start.9 = (f32[288,128]{1,0:T(8,128)S(1)}, f32[288,128]{1,0:T(8,128)S(1)}, u32[]{:S(2)}, u32[]{:S(2)}) collective-permute-start(f32[288,128]{1,0:T(8,128)S(1)} %pad_maximum_fusion.3), channel_id=1, source_target_pairs={{0,16},{2,18},{4,20},{6,22},{8,24},{10,26},{12,28},{14,30},{16,0},... | collective-permute-start | bytes 442376 | tf_op jit(solution)/shard_map/cond/branch_0_fun/cond/branch_1_fun/ppermute | solution.py:570
  151.9 9.7 %collective-permute-start.26 = (f32[256,128]{1,0:T(8,128)S(1)}, f32[256,128]{1,0:T(8,128)S(1)}, u32[]{:S(2)}, u32[]{:S(2)}) collective-permute-start(f32[256,128]{1,0:T(8,128)S(1)} %pad_maximum_fusion.5), channel_id=1, source_target_pairs={{0,1},{1,0},{2,3},{3,2},{4,5},{5,4},{6,7},{7,6},{8,9},{9,8},{10,11... | collective-permute-start | bytes 393224 | tf_op jit(solution)/shard_map/cond/branch_0_fun/ppermute | solution.py:556
  153.5 5.2 %copy-start.7 = (bf16[2048,128]{1,0:T(8,128)(2,1)}, bf16[2048,128]{1,0:T(8,128)(2,1)S(1)}, u32[]{:S(2)}) copy-start(bf16[2048,128]{1,0:T(8,128)(2,1)S(1)} %collective-permute-done.25.rest_0_.refs_3_) | copy-start | bytes 1572868 | tf_op jit(solution)/shard_map/cond
  162.3 2.1 collective-permute-start.14
  164.5 4.5 %collective-permute-start.15 = (f32[128,128]{1,0:T(8,128)S(1)}, f32[128,128]{1,0:T(8,128)S(1)}, u32[]{:S(2)}, u32[]{:S(2)}) collective-permute-start(f32[128,128]{1,0:T(8,128)S(1)} %constant_dynamic-slice_fusion.8), channel_id=1, source_target_pairs={{0,4},{2,6},{4,0},{6,2},{8,12},{10,14},{12,8},{14,10},{16,20},{18,... | collective-permute-start | bytes 196616 | tf_op jit(solution)/shard_map/cond/branch_0_fun/cond/branch_1_fun/ppermute | solution.py:570
  169.0 4.0 %collective-permute-start.16 = (f32[64,128]{1,0:T(8,128)S(1)}, f32[64,128]{1,0:T(8,128)S(1)}, u32[]{:S(2)}, u32[]{:S(2)}) collective-permute-start(f32[64,128]{1,0:T(8,128)S(1)} %constant_dynamic-slice_fusion.7), channel_id=1, source_target_pairs={{0,8},{2,10},{4,12},{6,14},{8,0},{10,2},{12,4},{14,6},{16,24},{18,... | collective-permute-start | bytes 98312 | tf_op jit(solution)/shard_map/cond/branch_0_fun/cond/branch_1_fun/ppermute | solution.py:570
  173.0 11.5 %collective-permute-start.17 = (f32[32,128]{1,0:T(8,128)S(1)}, f32[32,128]{1,0:T(8,128)S(1)}, u32[]{:S(2)}, u32[]{:S(2)}) collective-permute-start(f32[32,128]{1,0:T(8,128)S(1)} %constant_dynamic-slice_fusion.6), channel_id=1, source_target_pairs={{0,16},{2,18},{4,20},{6,22},{8,24},{10,26},{12,28},{14,30},{16,0},... | collective-permute-start | bytes 49160 | tf_op jit(solution)/shard_map/cond/branch_0_fun/cond/branch_1_fun/ppermute | solution.py:570
  186.1 4.9 %collective-permute-start.18 = (f32[32,256]{1,0:T(8,128)S(1)}, f32[32,256]{1,0:T(8,128)S(1)}, u32[]{:S(2)}, u32[]{:S(2)}) collective-permute-start(f32[32,256]{1,0:T(8,128)S(1)} %pad_maximum_fusion.4), channel_id=1, source_target_pairs={{0,16},{2,18},{4,20},{6,22},{8,24},{10,26},{12,28},{14,30},{16,0},... | collective-permute-start | bytes 98312 | tf_op jit(solution)/shard_map/cond/branch_0_fun/cond/branch_1_fun/ppermute | solution.py:570
  191.0 4.3 %collective-permute-start.19 = (f32[64,256]{1,0:T(8,128)S(1)}, f32[64,256]{1,0:T(8,128)S(1)}, u32[]{:S(2)}, u32[]{:S(2)}) collective-permute-start(f32[64,256]{1,0:T(8,128)S(1)} %maximum_select_fusion.3), channel_id=1, source_target_pairs={{0,8},{2,10},{4,12},{6,14},{8,0},{10,2},{12,4},{14,6},{16,24},{18,... | collective-permute-start | bytes 196616 | tf_op jit(solution)/shard_map/cond/branch_0_fun/cond/branch_1_fun/ppermute | solution.py:570
  195.3 5.0 %collective-permute-start.20 = (f32[128,256]{1,0:T(8,128)S(1)}, f32[128,256]{1,0:T(8,128)S(1)}, u32[]{:S(2)}, u32[]{:S(2)}) collective-permute-start(f32[128,256]{1,0:T(8,128)S(1)} %maximum_select_fusion.2), channel_id=1, source_target_pairs={{0,4},{2,6},{4,0},{6,2},{8,12},{10,14},{12,8},{14,10},{16,20},{18,... | collective-permute-start | bytes 393224 | tf_op jit(solution)/shard_map/cond/branch_0_fun/cond/branch_1_fun/ppermute | solution.py:570
  200.4 1.6 collective-permute-start.21
